TPU v7x, 512 devices: a whole 4x4x16 slice. The times are simulated.
512 devices in a mesh: row: 64 (over y, z), col: 8 (over x, core).
Axes of the slice: x: 4, y: 4, z: 16, core: 2. Of those that a mesh axis runs over, the one named last changes fastest.
Arguments:
- sketch: bfloat16 [65536, 128], P(('row', 'col')), may hold values from -6 to 6
- degree: float32 [65536], P(('row', 'col')), may hold values from 1 to 64
- block_vals: bfloat16 [64, 8, 16, 128, 128], P('row', 'col'), may hold values from -0.125 to 0.125
- block_rows: int32 [64, 8, 16], P('row', 'col'), may hold values from 0 to 7
- block_cols: int32 [64, 8, 16], P('row', 'col'), may hold values from 0 to 63
- live_count: int32 [64, 8], P('row', 'col'), may hold values from 2 to 16, as said below
Outputs:
- basis: float32 [65536, 128], P(('row', 'col'))
- factor: float32 [128, 128], replicated
Inputs may be any that keep to these rules, and one draw needn't show every extreme that they name: Slots at or past live_count of a device are ignored; some device has all 16 slots live.
All inputs are finite; a program needn't handle non-finite values.
Results may differ from a plain program's by a relative error of at most 0.003.
Values may be sent and summed in bfloat16 or wider, within the bound.
A program may use at most 64 MiB of HBM per device.

v0:
```python
import jax
import jax.numpy as jnp
from jax import lax
from jax.sharding import PartitionSpec as P


def local(sketch, degree, block_vals, block_rows, block_cols, live_count):
    rows_dev = sketch.shape[0]
    rank = sketch.shape[1]
    slots = block_vals.shape[2]
    blk = block_vals.shape[3]
    n_row = lax.axis_size("row")
    n_col = lax.axis_size("col")
    row_blocks = rows_dev * n_col // blk
    col_blocks = rows_dev * n_row // blk
    nodes = rows_dev * n_row * n_col
    values = block_vals.reshape(slots, blk, blk)
    rows_here = block_rows.reshape(slots)
    cols_here = block_cols.reshape(slots)
    live_total = live_count.reshape(())
    slot_ids = lax.iota(jnp.int32, slots)
    block_ids = lax.iota(jnp.int32, row_blocks)
    live = slot_ids < live_total
    table = ((rows_here[:, None] == block_ids[None, :]) & live[:, None]).astype(jnp.float32)
    scale = lax.rsqrt(degree)
    basis = sketch.astype(jnp.float32)
    moved = (scale[:, None] * basis).astype(jnp.bfloat16)
    stripe = lax.all_gather(moved, "row", axis=0, tiled=True)
    stripe_blocks = stripe.reshape(col_blocks, blk, rank)
    picked = jnp.take(stripe_blocks, cols_here, axis=0)
    products = jnp.einsum("nab,nbk->nak", values, picked, preferred_element_type=jnp.float32)
    partial_value = jnp.einsum("nr,nak->rak", table, products, precision=lax.Precision.HIGHEST)
    partial_value = partial_value.reshape(row_blocks * blk, rank)
    summed = lax.psum_scatter(partial_value, "col", scatter_dimension=0, tiled=True)
    image = scale[:, None] * summed
    local_gram = jnp.dot(image.T, image, precision=lax.Precision.HIGHEST)
    gram = lax.psum(local_gram, ("row", "col"))
    gram = gram / nodes
    lower = jnp.linalg.cholesky(gram)
    basis = jax.scipy.linalg.solve_triangular(lower, image.T, lower=True).T
    return (basis, lower.T)


def solution(mesh):
    in_specs = (
        P(("row", "col"), None),
        P(("row", "col")),
        P("row", "col", None, None, None),
        P("row", "col", None),
        P("row", "col", None),
        P("row", "col"),
    )
    out_specs = (P(("row", "col"), None), P())
    return jax.shard_map(local, mesh=mesh, in_specs=in_specs, out_specs=out_specs, check_vma=False)
```

profile of v0, /device:TPU:1, one launch (start us, length us, event | category | flops | bytes accessed | tf_op | source)
XLA Modules:
  0.0 684.9 jit_solution(11248738669199386243)
XLA Ops:
  7.2 0.0 copy-start
  7.2 0.0 all-gather.2.cloned.1.call-start
  7.2 0.7 rsqrt.3
  7.9 1.5 multiply_convert_fusion
  9.4 0.0 all-gather.2.cloned.1.call-update
  9.4 0.0 reduce-scatter.2.cloned.1.call-start
  10.1 0.7 fusion.21
  10.8 0.7 compare_and_fusion
  11.5 136.5 %all-gather.2.cloned.1.call-done = bf16[8192,128]{1,0:T(8,128)(2,1)} async-done(((bf16[128,128]{1,0:T(8,128)(2,1)}), bf16[8192,128]{1,0:T(8,128)(2,1)}) %all-gather.2.cloned.1.call-update) | async-done | bytes 2097168 | tf_op jit(solution)/shard_map/all_gather | solution.py:28
  148.0 2.2 gather_fusion
  150.2 0.0 copy-done
  150.3 0.0 copy-start.1
  150.3 0.7 fusion.2
  151.0 0.5 copy.15
  151.5 0.0 copy-done.1
  151.5 0.5 fusion
  152.0 0.9 copy.11
  152.9 0.0 reduce-scatter.2.cloned.1.call-update
  152.9 0.0 all-reduce.2.cloned.1.call-start
  152.9 43.5 %reduce-scatter.2.cloned.1.call-done = f32[128,128]{1,0:T(8,128)} async-done(((f32[1024,128]{1,0:T(8,128)}), f32[128,128]{1,0:T(8,128)}) %reduce-scatter.2.cloned.1.call-update) | async-done | bytes 65552 | tf_op jit(solution)/shard_map/reduce_scatter | solution.py:34
  196.4 1.9 fusion.11
  198.3 0.0 all-reduce.2.cloned.1.call-update
  198.4 452.9 %all-reduce.2.cloned.1.call-done = f32[128,128]{0,1:T(8,128)} async-done(((f32[128,128]{0,1:T(8,128)}), f32[128,128]{0,1:T(8,128)}) %all-reduce.2.cloned.1.call-update) | async-done | bytes 65552 | tf_op jit(solution)/shard_map/psum | solution.py:37
  651.2 0.8 broadcast_multiply_fusion
  652.1 0.1 copy.13
  652.1 0.9 fusion.9
  653.0 11.7 %cholesky.16 = f32[128,128]{1,0:T(8,128)S(1)} custom-call(f32[128,128]{1,0:T(8,128)S(1)} %fusion.9), custom_call_target="Cholesky" | custom-call | tf_op jit(solution)/shard_map/jit(cholesky)/cholesky | solution.py:39
  664.8 0.6 compare_reduce_fusion
  665.4 0.7 fusion.13
  666.1 9.8 %custom-call.7 = f32[1,128,128]{1,2,0:T(8,128)S(1)} custom-call(f32[1,128,128]{2,1,0:T(8,128)S(1)} %get-tuple-element.7), custom_call_target="InvertDiagBlocksLowerTriangular" | custom-call | tf_op jit(solution)/shard_map/jit(_solve_triangular)/triangular_solve | solution.py:40
  675.9 0.7 copy.14
  676.6 1.7 fusion.7
  (3 shorter events, 0.1 us)
Async XLA Ops:
  7.2 143.1 %copy-start = (bf16[1,1,16,128,128]{4,3,2,1,0:T(8,128)(2,1)S(1)}, bf16[1,1,16,128,128]{4,3,2,1,0:T(8,128)(2,1)}, u32[]{:S(2)}) copy-start(bf16[1,1,16,128,128]{4,3,2,1,0:T(8,128)(2,1)} %param.8) | copy-start | bytes 1572868
  7.2 140.8 %all-gather.2.cloned.1.call-start = ((), (), s32[]{:S(2)}) async-start(), calls=%async_computation.1 | async-start | bytes 2129920 | tf_op jit(solution)/shard_map/all_gather | solution.py:28
  9.4 187.0 %reduce-scatter.2.cloned.1.call-start = ((), (), s32[]{:S(2)}) async-start(), calls=%async_computation.2 | async-start | bytes 589824 | tf_op jit(solution)/shard_map/reduce_scatter | solution.py:34
  150.3 1.2 copy-start.1
  152.9 498.3 %all-reduce.2.cloned.1.call-start = ((), (), s32[]{:S(2)}) async-start(), calls=%async_computation.3 | async-start | bytes 131072 | tf_op jit(solution)/shard_map/psum | solution.py:37
Sparse Core Ops, SparseCore 0:
  11.5 136.4 all-gather.1
  153.0 43.3 reduce-scatter.1
  202.5 448.7 all-reduce.1
where the time goes:
time: 685 us
  waiting for transfers between devices  633 us (92%)
  other arithmetic  27.3 us (4%)
  between operations  14.5 us (2%)
    psum x1, waiting for transfers between devices, local(): gram = lax.psum(local_gram, ('row', 'col'))  453 us
    all_gather x1, waiting for transfers between devices, local(): stripe = lax.all_gather(moved, 'row', axis=0, tiled=True)  137 us
    reduce_scatter x1, waiting for transfers between devices, local(): lax.psum_scatter(partial_value, 'col', scatter_dimension=0, tiled=True)  43.5 us
  transfers between devices with their start and end apart: 3, of which 3 were waited for; matrix products, arithmetic and copies ran while one was open for 0% of the time, Pallas kernels for 0%

commit v1 on v0

--- a/solution.py
+++ b/solution.py
@@ -34,7 +34,7 @@
     summed = lax.psum_scatter(partial_value, "col", scatter_dimension=0, tiled=True)
     image = scale[:, None] * summed
     local_gram = jnp.dot(image.T, image, precision=lax.Precision.HIGHEST)
-    gram = lax.psum(local_gram, ("row", "col"))
+    gram = lax.psum(lax.psum(local_gram, "row"), "col")
     gram = gram / nodes
     lower = jnp.linalg.cholesky(gram)
     basis = jax.scipy.linalg.solve_triangular(lower, image.T, lower=True).T

time: 685 us -> 567 us (0.83)
  waiting for transfers between devices: 633 us -> 514 us
    psum x1 -> x2, waiting for transfers between devices: 453 us -> 334 us  [local(): gram = lax.psum(lax.psum(local_gram, 'row'), 'col')]
  transfers between devices with their start and end apart: 3 -> 4, of which waited for: 3 -> 4; matrix products, arithmetic and copies ran while one was open for 0% -> 0% of each run, Pallas kernels for 0% -> 0%
where the time goes in v1:
time: 567 us; the launch traced here: 566 us
  waiting for transfers between devices  514 us (91%)
  other arithmetic  27.4 us (5%)
  between operations  14.5 us (3%)
    psum x2, waiting for transfers between devices, local(): gram = lax.psum(lax.psum(local_gram, 'row'), 'col')  334 us
    all_gather x1, waiting for transfers between devices, local(): stripe = lax.all_gather(moved, 'row', axis=0, tiled=True)  137 us
    reduce_scatter x1, waiting for transfers between devices, local(): lax.psum_scatter(partial_value, 'col', scatter_dimension=0, tiled=True)  43.5 us
    another operation x3, other arithmetic, local(): lower = jnp.linalg.cholesky(gram)  12.4 us
  transfers between devices with their start and end apart: 4, of which 4 were waited for; matrix products, arithmetic and copies ran while one was open for 0% of the time, Pallas kernels for 0%

profile of v1, /device:TPU:1, one launch (start us, length us, event | category | flops | bytes accessed | tf_op | source)
XLA Modules:
  0.0 566.3 jit_solution(10675013685807354658)
XLA Ops:
  7.2 0.0 copy-start
  7.2 0.0 all-gather.2.cloned.1.call-start
  7.2 0.7 rsqrt.3
  7.9 1.5 multiply_convert_fusion
  9.4 0.0 all-gather.2.cloned.1.call-update
  9.4 0.0 reduce-scatter.2.cloned.1.call-start
  10.1 0.7 fusion.21
  10.8 0.7 compare_and_fusion
  11.5 136.5 %all-gather.2.cloned.1.call-done = bf16[8192,128]{1,0:T(8,128)(2,1)} async-done(((bf16[128,128]{1,0:T(8,128)(2,1)}), bf16[8192,128]{1,0:T(8,128)(2,1)}) %all-gather.2.cloned.1.call-update) | async-done | bytes 2097168 | tf_op jit(solution)/shard_map/all_gather | solution.py:28
  148.0 2.2 gather_fusion
  150.3 0.7 fusion.2
  151.0 0.5 copy.15
  151.5 0.5 fusion
  152.0 0.9 copy.11
  152.9 0.0 reduce-scatter.2.cloned.1.call-update
  152.9 0.0 all-reduce.3.cloned.1.call-start
  152.9 43.5 %reduce-scatter.2.cloned.1.call-done = f32[128,128]{1,0:T(8,128)} async-done(((f32[1024,128]{1,0:T(8,128)}), f32[128,128]{1,0:T(8,128)}) %reduce-scatter.2.cloned.1.call-update) | async-done | bytes 65552 | tf_op jit(solution)/shard_map/reduce_scatter | solution.py:34
  196.4 1.9 fusion.11
  198.3 0.0 all-reduce.3.cloned.1.call-update
  198.4 0.0 all-reduce.5.cloned.1.call-start
  198.4 253.6 %all-reduce.3.cloned.1.call-done = f32[128,128]{0,1:T(8,128)} async-done(((f32[128,128]{0,1:T(8,128)}), f32[128,128]{0,1:T(8,128)}) %all-reduce.3.cloned.1.call-update) | async-done | bytes 65552 | tf_op jit(solution)/shard_map/psum | solution.py:37
  452.1 0.0 all-reduce.5.cloned.1.call-update
  452.1 80.6 %all-reduce.5.cloned.1.call-done = f32[128,128]{0,1:T(8,128)} async-done(((f32[128,128]{0,1:T(8,128)}), f32[128,128]{0,1:T(8,128)}) %all-reduce.5.cloned.1.call-update) | async-done | bytes 65552 | tf_op jit(solution)/shard_map/psum | solution.py:37
  532.7 0.8 broadcast_multiply_fusion
  533.5 0.1 copy.13
  533.6 0.9 fusion.9
  534.5 11.7 %cholesky.16 = f32[128,128]{1,0:T(8,128)S(1)} custom-call(f32[128,128]{1,0:T(8,128)S(1)} %fusion.9), custom_call_target="Cholesky" | custom-call | tf_op jit(solution)/shard_map/jit(cholesky)/cholesky | solution.py:39
  546.2 0.6 compare_reduce_fusion
  546.9 0.7 fusion.13
  547.5 9.8 %custom-call.7 = f32[1,128,128]{1,2,0:T(8,128)S(1)} custom-call(f32[1,128,128]{2,1,0:T(8,128)S(1)} %get-tuple-element.7), custom_call_target="InvertDiagBlocksLowerTriangular" | custom-call | tf_op jit(solution)/shard_map/jit(_solve_triangular)/triangular_solve | solution.py:40
  557.3 0.7 copy.14
  558.1 1.7 fusion.7
  (6 shorter events, 0.1 us)
Async XLA Ops:
  7.2 143.1 %copy-start = (bf16[1,1,16,128,128]{4,3,2,1,0:T(8,128)(2,1)S(1)}, bf16[1,1,16,128,128]{4,3,2,1,0:T(8,128)(2,1)}, u32[]{:S(2)}) copy-start(bf16[1,1,16,128,128]{4,3,2,1,0:T(8,128)(2,1)} %param.8) | copy-start | bytes 1572868
  7.2 140.8 %all-gather.2.cloned.1.call-start = ((), (), s32[]{:S(2)}) async-start(), calls=%async_computation.1 | async-start | bytes 2129920 | tf_op jit(solution)/shard_map/all_gather | solution.py:28
  9.4 187.0 %reduce-scatter.2.cloned.1.call-start = ((), (), s32[]{:S(2)}) async-start(), calls=%async_computation.2 | async-start | bytes 589824 | tf_op jit(solution)/shard_map/reduce_scatter | solution.py:34
  150.3 1.2 copy-start.1
  152.9 299.2 %all-reduce.3.cloned.1.call-start = ((), (), s32[]{:S(2)}) async-start(), calls=%async_computation.3 | async-start | bytes 131072 | tf_op jit(solution)/shard_map/psum | solution.py:37
  198.4 334.3 %all-reduce.5.cloned.1.call-start = ((), (), s32[]{:S(2)}) async-start(), calls=%async_computation.4 | async-start | bytes 131072 | tf_op jit(solution)/shard_map/psum | solution.py:37
Sparse Core Ops, SparseCore 0:
  11.5 136.4 all-gather.1
  153.0 43.3 reduce-scatter.1
  200.4 251.5 all-reduce.2
  454.2 78.4 all-reduce.4

commit v2 on v0

--- a/solution.py
+++ b/solution.py
@@ -34,7 +34,7 @@
     summed = lax.psum_scatter(partial_value, "col", scatter_dimension=0, tiled=True)
     image = scale[:, None] * summed
     local_gram = jnp.dot(image.T, image, precision=lax.Precision.HIGHEST)
-    gram = lax.psum(local_gram, ("row", "col"))
+    gram = jnp.sum(lax.all_gather(local_gram, ("row", "col")), axis=0)
     gram = gram / nodes
     lower = jnp.linalg.cholesky(gram)
     basis = jax.scipy.linalg.solve_triangular(lower, image.T, lower=True).T

time: 685 us -> 484 us (0.71)
  waiting for transfers between devices: 633 us -> 421 us
  other arithmetic: 27.3 us -> 38.8 us
    psum x1 -> x0, waiting for transfers between devices: 453 us -> none  [local(): gram = lax.psum(local_gram, ('row', 'col'))]
    all_gather x0 -> x1, waiting for transfers between devices: none -> 241 us  [local(): gram = jnp.sum(lax.all_gather(local_gram, ('row', 'col')), axis=0)]
    reduce_sum x0 -> x1, other arithmetic: none -> 13.1 us  [local(): gram = jnp.sum(lax.all_gather(local_gram, ('row', 'col')), axis=0)]
where the time goes in v2:
time: 484 us
  waiting for transfers between devices  421 us (87%)
  other arithmetic  38.8 us (8%)
  between operations  14.5 us (3%)
  local copies, waits for them, and re-layouts  5.16 us (1%)
    all_gather x1, waiting for transfers between devices, local(): gram = jnp.sum(lax.all_gather(local_gram, ('row', 'col')), axis=0)  241 us
    all_gather x1, waiting for transfers between devices, local(): stripe = lax.all_gather(moved, 'row', axis=0, tiled=True)  137 us
    reduce_scatter x1, waiting for transfers between devices, local(): lax.psum_scatter(partial_value, 'col', scatter_dimension=0, tiled=True)  43.5 us
    reduce_sum x1, other arithmetic, local(): gram = jnp.sum(lax.all_gather(local_gram, ('row', 'col')), axis=0)  13.1 us
    another operation x3, other arithmetic, local(): lower = jnp.linalg.cholesky(gram)  12.4 us
    another operation x1, other arithmetic, local(): basis = jax.scipy.linalg.solve_triangular(lower, image.T, lower=True).T  9.81 us
  transfers between devices with their start and end apart: 3, of which 3 were waited for; matrix products, arithmetic and copies ran while one was open for 0% of the time, Pallas kernels for 0%

profile of v2, /device:TPU:1, one launch (start us, length us, event | category | flops | bytes accessed | tf_op | source)
XLA Modules:
  0.0 483.8 jit_solution(17389144522779388520)
XLA Ops:
  7.2 0.0 copy-start
  7.2 0.0 all-gather.4.cloned.1.call-start
  7.2 0.7 rsqrt.3
  7.9 1.5 multiply_convert_fusion
  9.4 0.0 all-gather.4.cloned.1.call-update
  9.4 0.0 reduce-scatter.2.cloned.1.call-start
  10.1 0.7 fusion.19
  10.8 0.7 compare_and_fusion
  11.5 136.5 %all-gather.4.cloned.1.call-done = bf16[8192,128]{1,0:T(8,128)(2,1)} async-done(((bf16[128,128]{1,0:T(8,128)(2,1)}), bf16[8192,128]{1,0:T(8,128)(2,1)}) %all-gather.4.cloned.1.call-update) | async-done | bytes 2097168 | tf_op jit(solution)/shard_map/all_gather | solution.py:28
  148.0 2.2 gather_fusion
  150.2 0.0 copy-done
  150.3 0.0 copy-start.2
  150.3 0.7 convolution_bitcast_fusion
  151.0 0.5 copy.18
  151.5 0.0 copy-done.2
  151.5 0.5 fusion.15
  152.0 0.9 copy.19
  152.8 0.0 reduce-scatter.2.cloned.1.call-update
  152.9 0.0 all-gather.6.cloned.1.call-start
  152.9 43.5 %reduce-scatter.2.cloned.1.call-done = f32[128,128]{1,0:T(8,128)} async-done(((f32[1024,128]{1,0:T(8,128)}), f32[128,128]{1,0:T(8,128)}) %reduce-scatter.2.cloned.1.call-update) | async-done | bytes 65552 | tf_op jit(solution)/shard_map/reduce_scatter | solution.py:34
  196.4 1.9 fusion.8
  198.3 0.0 all-gather.6.cloned.1.call-update
  198.3 241.2 %all-gather.6.cloned.1.call-done = f32[65536,128]{1,0:T(8,128)} async-done(((f32[128,128]{1,0:T(8,128)}), f32[65536,128]{1,0:T(8,128)}) %all-gather.6.cloned.1.call-update) | async-done | bytes 33554448 | tf_op jit(solution)/shard_map/all_gather | solution.py:37
  439.5 13.1 %reduce_sum.11 = f32[128,128]{1,0:T(8,128)S(1)} reduce(f32[512,128,128]{2,1,0:T(8,128)} %bitcast.32, f32[]{:T(128)} %constant.59.clone.1), dimensions={0}, to_apply=%region_1.2 | reduce | flops 8372224 | bytes 33619972 | tf_op jit(solution)/shard_map/reduce_sum | solution.py:37
  452.6 0.1 copy.20
  452.8 11.7 %cholesky.16 = f32[128,128]{1,0:T(8,128)S(1)} custom-call(f32[128,128]{1,0:T(8,128)S(1)} %fusion.6), custom_call_target="Cholesky" | custom-call | tf_op jit(solution)/shard_map/jit(cholesky)/cholesky | solution.py:39
  464.5 0.6 compare_reduce_fusion
  465.1 0.7 fusion.10
  465.8 0.7 copy.21
  466.5 9.8 %custom-call.7 = f32[1,128,128]{1,2,0:T(8,128)S(1)} custom-call(f32[1,128,128]{2,1,0:T(8,128)S(1)} %get-tuple-element.11), custom_call_target="InvertDiagBlocksLowerTriangular" | custom-call | tf_op jit(solution)/shard_map/jit(_solve_triangular)/triangular_solve | solution.py:40
  476.4 0.0 copy-done.1
  476.4 0.9 fusion.4
  (5 shorter events, 0.1 us)
Async XLA Ops:
  7.2 143.1 %copy-start = (bf16[1,1,16,128,128]{4,3,2,1,0:T(8,128)(2,1)S(1)}, bf16[1,1,16,128,128]{4,3,2,1,0:T(8,128)(2,1)}, u32[]{:S(2)}) copy-start(bf16[1,1,16,128,128]{4,3,2,1,0:T(8,128)(2,1)} %param.8) | copy-start | bytes 1572868
  7.2 140.8 %all-gather.4.cloned.1.call-start = ((), (), s32[]{:S(2)}) async-start(), calls=%async_computation.1 | async-start | bytes 2129920 | tf_op jit(solution)/shard_map/all_gather | solution.py:28
  9.4 187.0 %reduce-scatter.2.cloned.1.call-start = ((), (), s32[]{:S(2)}) async-start(), calls=%async_computation.2 | async-start | bytes 589824 | tf_op jit(solution)/shard_map/reduce_scatter | solution.py:34
  150.3 1.2 copy-start.2
  152.9 286.6 %all-gather.6.cloned.1.call-start = ((), (), s32[]{:S(2)}) async-start(), calls=%async_computation.3 | async-start | bytes 33619968 | tf_op jit(solution)/shard_map/all_gather | solution.py:37
  439.5 36.8 %copy-start.1 = (f32[128,128]{1,0:T(8,128)S(1)}, f32[128,128]{1,0:T(8,128)}, u32[]{:S(2)}) copy-start(f32[128,128]{1,0:T(8,128)} %reduce-scatter.2.cloned.1.call-done) | copy-start | bytes 196612
Sparse Core Ops, SparseCore 0:
  11.5 136.4 all-gather.3
  153.0 43.3 reduce-scatter.1
  201.5 238.0 all-gather.5
